TPU v7x, 256 devices: a whole 4x4x8 slice. The times are simulated.
256 devices in a mesh: section: 8 (over y, core), dp: 32 (over z, x).
Axes of the slice: x: 4, y: 4, z: 8, core: 2. Of those that a mesh axis runs over, the one named last changes fastest.
Arguments:
- crop_maps: bfloat16 [32, 4, 2, 8, 8, 640], P('dp'), may hold values from -6 to 6
- target_maps: int32 [32, 4, 2, 8, 8], P('dp'), may hold values 0 or 1
- crop_counts: int32 [32, 4], P('dp'), may hold values from 1 to 2, as said below
- depth_kernels: float32 [8, 49, 640], P('section'), may hold values from -0.875 to 0.875
- weight_in: bfloat16 [8, 640, 2560], P('section', 'dp'), may hold values from -0.25 to 0.25
- weight_out: bfloat16 [8, 2560, 640], P('section', 'dp'), may hold values from -0.125 to 0.125
- head_weight: float32 [640], replicated, may hold values from -0.25 to 0.25
Outputs:
- grad_in: float32 [8, 640, 2560], P('section', 'dp')
- grad_out: float32 [8, 2560, 640], P('section', 'dp')
- grad_kernels: float32 [8, 49, 640], P('section')
- grad_head: float32 [640], replicated
- loss_value: float32 [], replicated
Inputs may be any that keep to these rules, and one draw needn't show every extreme that they name: `crop_counts`: every data group has some micro-batch with exactly 2 crops.
All inputs are finite; a program needn't handle non-finite values. No bound on the sum of `target_maps` on one device may be relied on, other than what follows from the above.
Results may differ from a plain program's by a relative error of at most 0.034.
Values may be sent and summed in bfloat16 or wider, within the bound.
No kernel may reach another device: no remote copies, remote signals or barrier semaphores. Data moves between devices by JAX's collectives and lax.ppermute only.
A program may use at most 128 MiB of HBM per device.

v0:
```python
import jax
import jax.numpy as jnp
from jax import lax
from jax.sharding import PartitionSpec as P

EPSILON = 1e-06
SQRT_HALF = 0.7071067811865476
INV_ROOT_TWO_PI = 0.3989422804014327


def from_behind(value, axis, steps):
    count = lax.axis_size(axis)
    first, last = (max(0, -steps), min(count, count - steps))
    return lax.ppermute(value, axis, [(source, source + steps) for source in range(first, last)])


def depthwise(values, kernel):
    side = values.shape[1]
    padded = jnp.pad(values, ((0, 0), (3, 3), (3, 3), (0, 0)))
    result = jnp.zeros_like(values)
    for vertical in range(7):
        for across in range(7):
            result = (
                result
                + padded[:, vertical : vertical + side, across : across + side, :]
                * kernel[vertical * 7 + across]
            )
    return result


def depthwise_back(grads, kernel):
    side = grads.shape[1]
    padded = jnp.pad(grads, ((0, 0), (3, 3), (3, 3), (0, 0)))
    result = jnp.zeros_like(grads)
    for vertical in range(7):
        for across in range(7):
            result = (
                result
                + padded[:, 6 - vertical : 6 - vertical + side, 6 - across : 6 - across + side, :]
                * kernel[vertical * 7 + across]
            )
    return result


def kernel_grad(values, grads):
    side = values.shape[1]
    padded = jnp.pad(values, ((0, 0), (3, 3), (3, 3), (0, 0)))
    taps = []
    for vertical in range(7):
        for across in range(7):
            taps.append(
                jnp.sum(
                    padded[:, vertical : vertical + side, across : across + side, :] * grads,
                    axis=(0, 1, 2),
                )
            )
    return jnp.stack(taps, axis=0)


def block_parts(tiles, kernel, weight_in):
    width = tiles.shape[-1]
    widened = tiles.astype(jnp.float32)
    mixed = depthwise(widened, kernel).reshape(-1, width)
    centred = mixed - jnp.mean(mixed, axis=-1, keepdims=True)
    inverse = lax.rsqrt(jnp.mean(centred * centred, axis=-1, keepdims=True) + EPSILON)
    normed = centred * inverse
    normed_low = normed.astype(jnp.bfloat16)
    hidden = jnp.dot(normed_low, weight_in, preferred_element_type=jnp.float32)
    activated = (hidden * 0.5 * (1.0 + lax.erf(hidden * SQRT_HALF))).astype(jnp.bfloat16)
    return (widened, normed, inverse, normed_low, hidden, activated)


def block_forward(tiles, kernel, weight_in, weight_out):
    width = tiles.shape[-1]
    widened, normed, inverse, normed_low, hidden, activated = block_parts(tiles, kernel, weight_in)
    output = jnp.dot(activated, weight_out, preferred_element_type=jnp.float32)
    return (widened.reshape(-1, width) + output).astype(jnp.bfloat16).reshape(tiles.shape)


def block_backward(tiles, upstream, kernel, weight_in, weight_out):
    width = tiles.shape[-1]
    widened, normed, inverse, normed_low, hidden, activated = block_parts(tiles, kernel, weight_in)
    up_flat = upstream.reshape(-1, width)
    through = lax.dot_general(
        up_flat, weight_out, (((1,), (1,)), ((), ())), preferred_element_type=jnp.float32
    )
    slope = (
        0.5 * (1.0 + lax.erf(hidden * SQRT_HALF))
        + hidden * jnp.exp(-0.5 * hidden * hidden) * INV_ROOT_TWO_PI
    )
    hidden_grad = (through * slope).astype(jnp.bfloat16)
    normed_grad = lax.dot_general(
        hidden_grad, weight_in, (((1,), (1,)), ((), ())), preferred_element_type=jnp.float32
    )
    mixed_grad = inverse * (
        normed_grad
        - jnp.mean(normed_grad, axis=-1, keepdims=True)
        - normed * jnp.mean(normed_grad * normed, axis=-1, keepdims=True)
    )
    mixed_tiles = mixed_grad.reshape(tiles.shape)
    kernel_term = kernel_grad(widened, mixed_tiles)
    tile_grad = (upstream.astype(jnp.float32) + depthwise_back(mixed_tiles, kernel)).astype(
        jnp.bfloat16
    )
    return (tile_grad, kernel_term, normed_low, hidden_grad, activated, up_flat)


def outer_sum(left, right):
    return lax.dot_general(
        left, right, (((0,), (0,)), ((), ())), preferred_element_type=jnp.float32
    )


def head_terms(final, targets, live, head_weight, factor):
    widened = final.astype(jnp.float32)
    logits = jnp.sum(widened * head_weight, axis=-1)
    weight_live = live.astype(jnp.float32)[:, :, None, None]
    truth = targets.astype(jnp.float32)
    loss_term = jnp.sum(weight_live * (jax.nn.softplus(logits) - truth * logits)) * factor
    logit_grad = (jax.nn.sigmoid(logits) - truth) * weight_live * factor
    seeds = (logit_grad[..., None] * head_weight).astype(jnp.bfloat16)
    head_term = jnp.sum(logit_grad[..., None] * widened, axis=(0, 1, 2, 3))
    return (loss_term, seeds, head_term)


def body(crop_maps, target_maps, crop_counts, depth_kernels, weight_in, weight_out, head_weight):
    section_index = lax.axis_index("section")
    section_count = lax.axis_size("section")
    micro_count = crop_maps.shape[1]
    slot_count = crop_maps.shape[2]
    kernel = depth_kernels[0]
    live = jnp.arange(slot_count)[None, :] < crop_counts[0][:, None]
    entering = crop_maps[0] * live[:, :, None, None, None].astype(jnp.bfloat16)
    first_full, second_full = (
        lax.all_gather(weight_in[0], "dp", axis=0, tiled=True),
        lax.all_gather(weight_out[0], "dp", axis=0, tiled=True),
    )
    blank_tile = jnp.zeros(entering.shape[1:], jnp.bfloat16)
    ticks = micro_count + section_count - 1

    def forward_step(moment, carry):
        arrived, saved, final = carry
        micro = moment - section_index
        active = (micro >= 0) & (micro < micro_count)
        place = jnp.clip(micro, 0, micro_count - 1)
        own_tiles = lax.dynamic_index_in_dim(entering, place, 0, keepdims=False)
        current = jnp.where(section_index == 0, own_tiles, arrived)
        result = lax.cond(
            active,
            lambda tiles: block_forward(tiles, kernel, first_full, second_full),
            lambda tiles: jnp.zeros_like(tiles),
            current,
        )
        old_saved = lax.dynamic_index_in_dim(saved, place, 0, keepdims=False)
        saved = lax.dynamic_update_index_in_dim(
            saved, jnp.where(active, current, old_saved), place, 0
        )
        old_final = lax.dynamic_index_in_dim(final, place, 0, keepdims=False)
        final = lax.dynamic_update_index_in_dim(
            final, jnp.where(active, result, old_final), place, 0
        )
        arrived = from_behind(result, "section", 1)
        return (arrived, saved, final)

    _, saved, final = lax.fori_loop(
        0, ticks, forward_step, (blank_tile, jnp.zeros_like(entering), jnp.zeros_like(entering))
    )
    is_last = section_index == section_count - 1
    last_weight = is_last.astype(jnp.float32)
    factor = 1.0 / (micro_count * slot_count)
    loss_term, seeds, head_term = head_terms(final, target_maps[0], live, head_weight, factor)
    head_total, loss_total = lax.psum(
        (head_term * last_weight, loss_term * last_weight), ("section", "dp")
    )
    first_back, second_back = (
        lax.all_gather(weight_in[0], "dp", axis=0, tiled=True),
        lax.all_gather(weight_out[0], "dp", axis=0, tiled=True),
    )
    width = entering.shape[-1]
    expand = first_back.shape[1]
    extra_start = (jnp.zeros((width, expand), jnp.float32), jnp.zeros((expand, width), jnp.float32))

    def backward_step(moment, carry):
        arrived, kernel_acc, extra = carry
        micro = moment - (section_count - 1 - section_index)
        active = (micro >= 0) & (micro < micro_count)
        place = jnp.clip(micro, 0, micro_count - 1)
        own_seed = lax.dynamic_index_in_dim(seeds, place, 0, keepdims=False)
        upstream = jnp.where(is_last, own_seed, arrived)
        stored = lax.dynamic_index_in_dim(saved, place, 0, keepdims=False)

        def run_block(operands):
            grad_tiles, inputs, acc_kernel, acc_extra = operands
            tile_grad, kernel_term, normed_low, hidden_grad, activated, up_flat = block_backward(
                inputs, grad_tiles, kernel, first_back, second_back
            )
            new_extra = (
                acc_extra[0] + outer_sum(normed_low, hidden_grad),
                acc_extra[1] + outer_sum(activated, up_flat),
            )
            return (tile_grad, acc_kernel + kernel_term, new_extra)

        def skip_block(operands):
            return (jnp.zeros_like(operands[0]), operands[2], operands[3])

        tile_grad, kernel_acc, extra = lax.cond(
            active, run_block, skip_block, (upstream, stored, kernel_acc, extra)
        )
        arrived = from_behind(tile_grad, "section", -1)
        return (arrived, kernel_acc, extra)

    _, kernel_acc, extra = lax.fori_loop(
        0, ticks, backward_step, (blank_tile, jnp.zeros(kernel.shape, jnp.float32), extra_start)
    )
    first_part, second_part = (
        lax.psum_scatter(
            extra[0].astype(jnp.bfloat16), "dp", scatter_dimension=0, tiled=True
        ).astype(jnp.float32),
        lax.psum_scatter(
            extra[1].astype(jnp.bfloat16), "dp", scatter_dimension=0, tiled=True
        ).astype(jnp.float32),
    )
    kernel_total = lax.psum(kernel_acc.astype(jnp.bfloat16), "dp").astype(jnp.float32)
    return (first_part[None], second_part[None], kernel_total[None], head_total, loss_total)


def solution(mesh):
    return jax.shard_map(
        body,
        mesh=mesh,
        in_specs=(
            P("dp", None, None, None, None, None),
            P("dp", None, None, None, None),
            P("dp", None),
            P("section", None, None),
            P("section", "dp", None),
            P("section", "dp", None),
            P(),
        ),
        out_specs=(
            P("section", "dp", None),
            P("section", "dp", None),
            P("section", None, None),
            P(),
            P(),
        ),
        check_vma=False,
    )
```

profile of v0, /device:TPU:1, one launch (start us, length us, event | category | flops | bytes accessed | tf_op | source)
XLA Modules:
  0.0 1533.0 jit_solution(5656709828315738469)
XLA Ops:
  13.1 91.3 %all-gather.5.cloned.1.call-done = bf16[1,640,2560]{2,0,1:T(2,128)(2,1)} async-done(((bf16[1,20,2560]{2,0,1:T(2,128)(2,1)}), bf16[1,640,2560]{2,0,1:T(2,128)(2,1)}) %all-gather.5.cloned.1.call-update) | async-done | bytes 3276816 | tf_op jit(solution)/shard_map/all_gather | solution.py:135
  108.0 72.7 %all-gather.7.cloned.1.call-done = bf16[1,2560,640]{2,1,0:T(8,128)(2,1)} async-done(((bf16[1,80,640]{2,1,0:T(8,128)(2,1)}), bf16[1,2560,640]{2,1,0:T(8,128)(2,1)}) %all-gather.7.cloned.1.call-update) | async-done | bytes 3276816 | tf_op jit(solution)/shard_map/all_gather | solution.py:136
  183.2 210.7 %while.40 = (s32[]{:T(128)}, bf16[2,8,8,640]{3,2,1,0:T(8,128)(2,1)}, bf16[4,2,8,8,640]{4,3,2,1,0:T(8,128)(2,1)}, bf16[4,2,8,8,640]{4,3,2,1,0:T(8,128)(2,1)}, s32...) while((s32[]{:T(128)}, ...), condition=%wide.region_5.6_spmd, body=%wide.region_0.5_spmd.sunk | while | flops 849510528 | bytes 13491009 | solution.py:165
  195.4 12.2 collective-permute-done
  210.3 14.7 conditional.5
  231.9 14.7 conditional.5
  256.1 14.7 conditional.5
  280.3 14.7 conditional.5
  304.5 19.2 %collective-permute-start = (bf16[2,8,8,640]{3,2,1,0:T(8,128)(2,1)S(1)}, bf16[2,8,8,640]{3,2,1,0:T(8,128)(2,1)}, u32[]{:S(2)}, u32[]{:S(2)}) collective-permute-start(bf16[2,8,8,640]{3,2,1,0:T(8,128)(2,1)S(1)} %get-tuple-element.1153), channel_id=1, source_target_pairs={{0,32},{32,64},{64,96},{96,128},{128,160},{160,192},{192,224},{1,3... | collective-permute-start | bytes 491528 | tf_op jit(solution)/shard_map/while/body/eval_jaxpr/ppermute | solution.py:14
  338.2 12.7 collective-permute-start
  365.5 16.6 %collective-permute-start = (bf16[2,8,8,640]{3,2,1,0:T(8,128)(2,1)S(1)}, bf16[2,8,8,640]{3,2,1,0:T(8,128)(2,1)}, u32[]{:S(2)}, u32[]{:S(2)}) collective-permute-start(bf16[2,8,8,640]{3,2,1,0:T(8,128)(2,1)S(1)} %get-tuple-element.1153), channel_id=1, source_target_pairs={{0,32},{32,64},{64,96},{96,128},{128,160},{160,192},{192,224},{1,3... | collective-permute-start | bytes 491528 | tf_op jit(solution)/shard_map/while/body/eval_jaxpr/ppermute | solution.py:14
  403.2 778.2 %while.41 = (s32[]{:T(128)}, bf16[2,8,8,640]{3,2,1,0:T(8,128)(2,1)}, f32[49,640]{1,0:T(8,128)S(1)}, f32[640,2560]{1,0:T(8,128)}, f32[2560,640]{1,0:T(8,128)}, /*...) while((s32[]{:T(128)}, ...), condition=%wide.region_63.64_spmd.clone, body=%wide.region_7.63_spmd.clone.sunk | while | flops 2131804288 | bytes 130983528 | solution.py:212
  407.5 14.1 collective-permute-done.1
  435.2 17.3 %collective-permute-done.1 = bf16[2,8,8,640]{3,2,1,0:T(8,128)(2,1)} collective-permute-done((bf16[2,8,8,640]{3,2,1,0:T(8,128)(2,1)}, bf16[2,8,8,640]{3,2,1,0:T(8,128)(2,1)}, u32[]{:S(2)}, u32[]{:S(2)}) %collective-permute-start.1) | collective-permute-done | bytes 163872 | tf_op jit(solution)/shard_map/while/body/eval_jaxpr/ppermute | solution.py:14
  466.1 13.4 collective-permute-done.1
  483.8 359.0 %collective-permute-done.1 = bf16[2,8,8,640]{3,2,1,0:T(8,128)(2,1)} collective-permute-done((bf16[2,8,8,640]{3,2,1,0:T(8,128)(2,1)}, bf16[2,8,8,640]{3,2,1,0:T(8,128)(2,1)}, u32[]{:S(2)}, u32[]{:S(2)}) %collective-permute-start.1) | collective-permute-done | bytes 163872 | tf_op jit(solution)/shard_map/while/body/eval_jaxpr/ppermute | solution.py:14
  844.6 60.5 %conditional.6 = (bf16[2,8,8,640]{3,2,1,0:T(8,128)(2,1)}, f32[49,640]{1,0:T(8,128)S(1)}, f32[640,2560]{1,0:T(8,128)}, f32[2560,640]{1,0:T(8,128)}) conditional(s32[]{:T(128)} %convert_element_type.175, (f32[49,640]{1,0:T(8,128)S(1)}, f32[640,2560]{1,0:T(8,128)}, f32[2560,640]{1,0:T(8,128)}) %tuple.251, (pred[]{:T(512)}, s32[]{:T(128)}, ...), branch_computations={%region_8.8_spmd, %region_9.62_spmd} | conditional | flops 2131148928 | bytes 129667864 | solution.py:206
  913.7 60.5 %conditional.6 = (bf16[2,8,8,640]{3,2,1,0:T(8,128)(2,1)}, f32[49,640]{1,0:T(8,128)S(1)}, f32[640,2560]{1,0:T(8,128)}, f32[2560,640]{1,0:T(8,128)}) conditional(s32[]{:T(128)} %convert_element_type.175, (f32[49,640]{1,0:T(8,128)S(1)}, f32[640,2560]{1,0:T(8,128)}, f32[2560,640]{1,0:T(8,128)}) %tuple.251, (pred[]{:T(512)}, s32[]{:T(128)}, ...), branch_computations={%region_8.8_spmd, %region_9.62_spmd} | conditional | flops 2131148928 | bytes 129667864 | solution.py:206
  982.8 60.5 %conditional.6 = (bf16[2,8,8,640]{3,2,1,0:T(8,128)(2,1)}, f32[49,640]{1,0:T(8,128)S(1)}, f32[640,2560]{1,0:T(8,128)}, f32[2560,640]{1,0:T(8,128)}) conditional(s32[]{:T(128)} %convert_element_type.175, (f32[49,640]{1,0:T(8,128)S(1)}, f32[640,2560]{1,0:T(8,128)}, f32[2560,640]{1,0:T(8,128)}) %tuple.251, (pred[]{:T(512)}, s32[]{:T(128)}, ...), branch_computations={%region_8.8_spmd, %region_9.62_spmd} | conditional | flops 2131148928 | bytes 129667864 | solution.py:206
  1051.9 60.5 %conditional.6 = (bf16[2,8,8,640]{3,2,1,0:T(8,128)(2,1)}, f32[49,640]{1,0:T(8,128)S(1)}, f32[640,2560]{1,0:T(8,128)}, f32[2560,640]{1,0:T(8,128)}) conditional(s32[]{:T(128)} %convert_element_type.175, (f32[49,640]{1,0:T(8,128)S(1)}, f32[640,2560]{1,0:T(8,128)}, f32[2560,640]{1,0:T(8,128)}) %tuple.251, (pred[]{:T(512)}, s32[]{:T(128)}, ...), branch_computations={%region_8.8_spmd, %region_9.62_spmd} | conditional | flops 2131148928 | bytes 129667864 | solution.py:206
  1121.6 58.4 %collective-permute-start.1 = (bf16[2,8,8,640]{3,2,1,0:T(8,128)(2,1)}, bf16[2,8,8,640]{3,2,1,0:T(8,128)(2,1)}, u32[]{:S(2)}, u32[]{:S(2)}) collective-permute-start(bf16[2,8,8,640]{3,2,1,0:T(8,128)(2,1)} %get-tuple-element.1051), channel_id=1, source_target_pairs={{32,0},{64,32},{96,64},{128,96},{160,128},{192,160},{224,192},{33,... | collective-permute-start | bytes 491528 | tf_op jit(solution)/shard_map/while/body/eval_jaxpr/ppermute | solution.py:14
  1191.4 84.2 %fusion.2 = bf16[24,2560]{1,0:T(8,128)(2,1)} fusion(bf16[640,2560]{1,0:T(8,128)(2,1)S(1)} %convert_element_type.133), kind=kCustom, calls=%all-reduce-scatter | all-reduce-scatter fusion | flops 1966081 | bytes 3400704
  1294.3 110.5 %psum.21 = bf16[1,49,640]{2,0,1:T(2,128)(2,1)S(1)} all-reduce(bf16[1,49,640]{2,0,1:T(2,128)(2,1)S(1)} %broadcast_in_dim.64), channel_id=1, replica_groups=mesh['section'=8,'dp'=32] {'dp'}, use_global_device_ids=true, to_apply=%region_66.67 | all-reduce | flops 31360 | bytes 125440 | tf_op jit(solution)/shard_map/psum | solution.py:223
  1406.9 115.7 %all-reduce.5 = (f32[640]{0:T(1024)}, f32[]{:T(128)}) all-reduce(f32[640]{0:T(1024)S(1)} %broadcast_multiply_fusion.4, f32[]{:T(128)S(6)} %mul.2377), channel_id=1, replica_groups=mesh['section'=8,'dp'=32] {'section','dp'}, use_global_device_ids=true, to_apply=%region_68.69 | all-reduce | flops 641 | bytes 5128 | tf_op jit(solution)/shard_map/psum | solution.py:172
  (1176 shorter events, 519.7 us)
Async XLA Ops:
  7.2 97.2 %all-gather.5.cloned.1.call-start = ((), (), s32[]{:S(2)}) async-start(), calls=%async_computation.2 | async-start | bytes 6758400 | tf_op jit(solution)/shard_map/all_gather | solution.py:135
  9.0 171.6 %all-gather.7.cloned.1.call-start = ((), (), s32[]{:S(2)}) async-start(), calls=%async_computation.3 | async-start | bytes 3379200 | tf_op jit(solution)/shard_map/all_gather | solution.py:136
  9.8 1515.1 %reduce-scatter.4.cloned.1.call-start = ((), (), s32[]{:S(2)}) async-start(), calls=%async_computation.1 | async-start | bytes 3379200 | tf_op jit(solution)/shard_map/reduce_scatter | solution.py:219
  185.9 21.6 %collective-permute-start = (bf16[2,8,8,640]{3,2,1,0:T(8,128)(2,1)S(1)}, bf16[2,8,8,640]{3,2,1,0:T(8,128)(2,1)}, u32[]{:S(2)}, u32[]{:S(2)}) collective-permute-start(bf16[2,8,8,640]{3,2,1,0:T(8,128)(2,1)S(1)} %get-tuple-element.1153), channel_id=1, source_target_pairs={{0,32},{32,64},{64,96},{96,128},{128,160},{160,192},{192,224},{1,3... | collective-permute-start | bytes 491528 | tf_op jit(solution)/shard_map/while/body/eval_jaxpr/ppermute | solution.py:14
  304.5 21.4 %collective-permute-start = (bf16[2,8,8,640]{3,2,1,0:T(8,128)(2,1)S(1)}, bf16[2,8,8,640]{3,2,1,0:T(8,128)(2,1)}, u32[]{:S(2)}, u32[]{:S(2)}) collective-permute-start(bf16[2,8,8,640]{3,2,1,0:T(8,128)(2,1)S(1)} %get-tuple-element.1153), channel_id=1, source_target_pairs={{0,32},{32,64},{64,96},{96,128},{128,160},{160,192},{192,224},{1,3... | collective-permute-start | bytes 491528 | tf_op jit(solution)/shard_map/while/body/eval_jaxpr/ppermute | solution.py:14
  338.2 14.9 collective-permute-start
  365.5 18.8 %collective-permute-start = (bf16[2,8,8,640]{3,2,1,0:T(8,128)(2,1)S(1)}, bf16[2,8,8,640]{3,2,1,0:T(8,128)(2,1)}, u32[]{:S(2)}, u32[]{:S(2)}) collective-permute-start(bf16[2,8,8,640]{3,2,1,0:T(8,128)(2,1)S(1)} %get-tuple-element.1153), channel_id=1, source_target_pairs={{0,32},{32,64},{64,96},{96,128},{128,160},{160,192},{192,224},{1,3... | collective-permute-start | bytes 491528 | tf_op jit(solution)/shard_map/while/body/eval_jaxpr/ppermute | solution.py:14
  405.6 16.0 %collective-permute-start.1 = (bf16[2,8,8,640]{3,2,1,0:T(8,128)(2,1)}, bf16[2,8,8,640]{3,2,1,0:T(8,128)(2,1)}, u32[]{:S(2)}, u32[]{:S(2)}) collective-permute-start(bf16[2,8,8,640]{3,2,1,0:T(8,128)(2,1)} %get-tuple-element.1051), channel_id=1, source_target_pairs={{32,0},{64,32},{96,64},{128,96},{160,128},{192,160},{224,192},{33,... | collective-permute-start | bytes 491528 | tf_op jit(solution)/shard_map/while/body/eval_jaxpr/ppermute | solution.py:14
  423.9 6.9 collective-permute-start.1
  433.3 19.2 %collective-permute-start.1 = (bf16[2,8,8,640]{3,2,1,0:T(8,128)(2,1)}, bf16[2,8,8,640]{3,2,1,0:T(8,128)(2,1)}, u32[]{:S(2)}, u32[]{:S(2)}) collective-permute-start(bf16[2,8,8,640]{3,2,1,0:T(8,128)(2,1)} %get-tuple-element.1051), channel_id=1, source_target_pairs={{32,0},{64,32},{96,64},{128,96},{160,128},{192,160},{224,192},{33,... | collective-permute-start | bytes 491528 | tf_op jit(solution)/shard_map/while/body/eval_jaxpr/ppermute | solution.py:14
  454.9 6.9 collective-permute-start.1
  464.2 15.3 %collective-permute-start.1 = (bf16[2,8,8,640]{3,2,1,0:T(8,128)(2,1)}, bf16[2,8,8,640]{3,2,1,0:T(8,128)(2,1)}, u32[]{:S(2)}, u32[]{:S(2)}) collective-permute-start(bf16[2,8,8,640]{3,2,1,0:T(8,128)(2,1)} %get-tuple-element.1051), channel_id=1, source_target_pairs={{32,0},{64,32},{96,64},{128,96},{160,128},{192,160},{224,192},{33,... | collective-permute-start | bytes 491528 | tf_op jit(solution)/shard_map/while/body/eval_jaxpr/ppermute | solution.py:14
  481.9 361.0 %collective-permute-start.1 = (bf16[2,8,8,640]{3,2,1,0:T(8,128)(2,1)}, bf16[2,8,8,640]{3,2,1,0:T(8,128)(2,1)}, u32[]{:S(2)}, u32[]{:S(2)}) collective-permute-start(bf16[2,8,8,640]{3,2,1,0:T(8,128)(2,1)} %get-tuple-element.1051), channel_id=1, source_target_pairs={{32,0},{64,32},{96,64},{128,96},{160,128},{192,160},{224,192},{33,... | collective-permute-start | bytes 491528 | tf_op jit(solution)/shard_map/while/body/eval_jaxpr/ppermute | solution.py:14
  905.0 6.9 collective-permute-start.1
  974.1 6.9 collective-permute-start.1
  1043.2 6.9 collective-permute-start.1
  1112.3 6.9 collective-permute-start.1
  1121.6 59.7 %collective-permute-start.1 = (bf16[2,8,8,640]{3,2,1,0:T(8,128)(2,1)}, bf16[2,8,8,640]{3,2,1,0:T(8,128)(2,1)}, u32[]{:S(2)}, u32[]{:S(2)}) collective-permute-start(bf16[2,8,8,640]{3,2,1,0:T(8,128)(2,1)} %get-tuple-element.1051), channel_id=1, source_target_pairs={{32,0},{64,32},{96,64},{128,96},{160,128},{192,160},{224,192},{33,... | collective-permute-start | bytes 491528 | tf_op jit(solution)/shard_map/while/body/eval_jaxpr/ppermute | solution.py:14
  1276.5 246.1 %collective-permute-start.6 = (bf16[24,2560]{1,0:T(8,128)(2,1)}, bf16[24,2560]{1,0:T(8,128)(2,1)S(1)}, u32[]{:S(2)}, u32[]{:S(2)}) collective-permute-start(bf16[24,2560]{1,0:T(8,128)(2,1)} %fusion.2), channel_id=1, source_target_pairs={{0,5},{1,6},{2,7},{3,8},{4,9},{5,10},{6,11},{7,12},{8,13},{9,14},{... | collective-permute-start | bytes 368648
  1277.8 244.8 %collective-permute-start.5 = (bf16[24,2560]{1,0:T(8,128)(2,1)}, bf16[24,2560]{1,0:T(8,128)(2,1)S(1)}, u32[]{:S(2)}, u32[]{:S(2)}) collective-permute-start(bf16[24,2560]{1,0:T(8,128)(2,1)} %fusion.2), channel_id=1, source_target_pairs={{0,4},{1,5},{2,6},{3,7},{4,8},{5,9},{6,10},{7,11},{8,12},{9,13},{1... | collective-permute-start | bytes 368648
  1279.3 243.3 %collective-permute-start.4 = (bf16[24,2560]{1,0:T(8,128)(2,1)}, bf16[24,2560]{1,0:T(8,128)(2,1)S(1)}, u32[]{:S(2)}, u32[]{:S(2)}) collective-permute-start(bf16[24,2560]{1,0:T(8,128)(2,1)} %fusion.2), channel_id=1, source_target_pairs={{0,3},{1,4},{2,5},{3,6},{4,7},{5,8},{6,9},{7,10},{8,11},{9,12},{10... | collective-permute-start | bytes 368648
  1280.6 242.0 %collective-permute-start.3 = (bf16[24,2560]{1,0:T(8,128)(2,1)}, bf16[24,2560]{1,0:T(8,128)(2,1)S(1)}, u32[]{:S(2)}, u32[]{:S(2)}) collective-permute-start(bf16[24,2560]{1,0:T(8,128)(2,1)} %fusion.2), channel_id=1, source_target_pairs={{0,2},{1,3},{2,4},{3,5},{4,6},{5,7},{6,8},{7,9},{8,10},{9,11},{10,... | collective-permute-start | bytes 368648
  1283.4 122.2 %collective-permute-start.7 = (bf16[4,2560]{1,0:T(4,128)(2,1)S(1)}, bf16[4,2560]{1,0:T(4,128)(2,1)S(1)}, u32[]{:S(2)}, u32[]{:S(2)}) collective-permute-start(bf16[4,2560]{1,0:T(4,128)(2,1)S(1)} %slice.1262), channel_id=1, source_target_pairs={{0,6},{1,7},{2,8},{3,9},{4,10},{5,11},{6,12},{7,13},{8,14},{9,15},... | collective-permute-start | bytes 61448
  1405.6 117.0 %collective-permute-start.2 = (bf16[24,2560]{1,0:T(8,128)(2,1)S(1)}, bf16[24,2560]{1,0:T(8,128)(2,1)S(1)}, u32[]{:S(2)}, u32[]{:S(2)}) collective-permute-start(bf16[24,2560]{1,0:T(8,128)(2,1)S(1)} %copy-done.77), channel_id=1, source_target_pairs={{0,1},{1,2},{2,3},{3,4},{4,5},{5,6},{6,7},{7,8},{8,9},{9,10},{10,1... | collective-permute-start | bytes 368648
  (339 other events, 1249.0 us)
Sparse Core Ops, SparseCore 0:
  11.2 93.1 all-gather.4
  107.0 73.6 all-gather.6
  1186.4 193.5 reduce-scatter.3
where the time goes:
time: 1540 us; the launch traced here: 1530 us
  waiting for transfers between devices  618 us (40%)
  blocking collectives  310 us (20%)
  local copies, waits for them, and re-layouts  199 us (13%)
  starting transfers between devices  180 us (12%)
  other arithmetic  145 us (9%)
  matrix products  59.4 us (4%)
    ppermute x22, waiting for transfers between devices, from_behind(): lax.ppermute(value, axis, [(source, source + steps) for source in range(f...  453 us
    ppermute x22, starting transfers between devices, from_behind(): lax.ppermute(value, axis, [(source, source + steps) for source in range(f...  163 us
    psum x1, blocking collectives, body(): lax.psum((head_term * last_weight, loss_term * last_weight), ('section',...  116 us
    psum x1, blocking collectives, body(): lax.psum(kernel_acc.astype(jnp.bfloat16), 'dp').astype(jnp.float32)  111 us
    another operation x200, local copies, waits for them, and re-layouts, kernel_grad(): return jnp.stack(taps, axis=0)  105 us
    all_gather x1, waiting for transfers between devices, body(): lax.all_gather(weight_in[0], 'dp', axis=0, tiled=True)  91.3 us
    unnamed x1, blocking collectives  84.2 us
    all_gather x1, waiting for transfers between devices, body(): lax.all_gather(weight_out[0], 'dp', axis=0, tiled=True)  72.7 us
  transfers between devices with their start and end apart: 31, of which 24 were waited for; matrix products, arithmetic and copies ran while one was open for 8% of the time, Pallas kernels for 0%

commit v1 on v0

--- a/solution.py
+++ b/solution.py
@@ -6,6 +6,11 @@
 EPSILON = 1e-06
 SQRT_HALF = 0.7071067811865476
 INV_ROOT_TWO_PI = 0.3989422804014327
+
+
+def feed_modes_here(a0):
+    mixed_arr = lax.psum(a0, "section")
+    return lax.psum(mixed_arr, "dp")
 
 
 def from_behind(value, axis, steps):
@@ -169,9 +174,7 @@
     last_weight = is_last.astype(jnp.float32)
     factor = 1.0 / (micro_count * slot_count)
     loss_term, seeds, head_term = head_terms(final, target_maps[0], live, head_weight, factor)
-    head_total, loss_total = lax.psum(
-        (head_term * last_weight, loss_term * last_weight), ("section", "dp")
-    )
+    head_total, loss_total = feed_modes_here((head_term * last_weight, loss_term * last_weight))
     first_back, second_back = (
         lax.all_gather(weight_in[0], "dp", axis=0, tiled=True),
         lax.all_gather(weight_out[0], "dp", axis=0, tiled=True),

time: 1540 us -> 1550 us (level)
    psum x1 -> x2, blocking collectives: 116 us -> 112 us  [the longest x1 57.4 us: feed_modes_here(): return lax.psum(mixed_arr, 'dp')]
where the time goes in v1:
time: 1550 us; the launch traced here: 1530 us
  waiting for transfers between devices  618 us (40%)
  blocking collectives  306 us (20%)
  local copies, waits for them, and re-layouts  199 us (13%)
  starting transfers between devices  181 us (12%)
  other arithmetic  145 us (9%)
  matrix products  59.4 us (4%)
    ppermute x22, waiting for transfers between devices, from_behind(): lax.ppermute(value, axis, [(source, source + steps) for source in range(f...  453 us
    ppermute x22, starting transfers between devices, from_behind(): lax.ppermute(value, axis, [(source, source + steps) for source in range(f...  163 us
    psum x1, blocking collectives, body(): lax.psum(kernel_acc.astype(jnp.bfloat16), 'dp').astype(jnp.float32)  111 us
    another operation x200, local copies, waits for them, and re-layouts, kernel_grad(): return jnp.stack(taps, axis=0)  105 us
    all_gather x1, waiting for transfers between devices, body(): lax.all_gather(weight_in[0], 'dp', axis=0, tiled=True)  91.3 us
    unnamed x1, blocking collectives  83.6 us
    all_gather x1, waiting for transfers between devices, body(): lax.all_gather(weight_out[0], 'dp', axis=0, tiled=True)  72.7 us
    psum x1, blocking collectives, feed_modes_here(): return lax.psum(mixed_arr, 'dp')  57.4 us
  transfers between devices with their start and end apart: 31, of which 24 were waited for; matrix products, arithmetic and copies ran while one was open for 8% of the time, Pallas kernels for 0%

profile of v1, /device:TPU:1, one launch (start us, length us, event | category | flops | bytes accessed | tf_op | source)
XLA Modules:
  0.0 1530.6 jit_solution(1258487595599113366)
XLA Ops:
  13.1 91.3 %all-gather.5.cloned.1.call-done = bf16[1,640,2560]{2,0,1:T(2,128)(2,1)} async-done(((bf16[1,20,2560]{2,0,1:T(2,128)(2,1)}), bf16[1,640,2560]{2,0,1:T(2,128)(2,1)}) %all-gather.5.cloned.1.call-update) | async-done | bytes 3276816 | tf_op jit(solution)/shard_map/all_gather | solution.py:140
  108.0 72.7 %all-gather.7.cloned.1.call-done = bf16[1,2560,640]{2,1,0:T(8,128)(2,1)} async-done(((bf16[1,80,640]{2,1,0:T(8,128)(2,1)}), bf16[1,2560,640]{2,1,0:T(8,128)(2,1)}) %all-gather.7.cloned.1.call-update) | async-done | bytes 3276816 | tf_op jit(solution)/shard_map/all_gather | solution.py:141
  183.2 210.7 %while.40 = (s32[]{:T(128)}, bf16[2,8,8,640]{3,2,1,0:T(8,128)(2,1)}, bf16[4,2,8,8,640]{4,3,2,1,0:T(8,128)(2,1)}, bf16[4,2,8,8,640]{4,3,2,1,0:T(8,128)(2,1)}, s32...) while((s32[]{:T(128)}, ...), condition=%wide.region_5.6_spmd, body=%wide.region_0.5_spmd.sunk | while | flops 849510528 | bytes 13491009 | solution.py:170
  210.3 14.7 conditional.5
  231.9 14.7 conditional.5
  256.1 14.7 conditional.5
  280.3 14.7 conditional.5
  304.5 19.2 %collective-permute-start = (bf16[2,8,8,640]{3,2,1,0:T(8,128)(2,1)S(1)}, bf16[2,8,8,640]{3,2,1,0:T(8,128)(2,1)}, u32[]{:S(2)}, u32[]{:S(2)}) collective-permute-start(bf16[2,8,8,640]{3,2,1,0:T(8,128)(2,1)S(1)} %get-tuple-element.1155), channel_id=1, source_target_pairs={{0,32},{32,64},{64,96},{96,128},{128,160},{160,192},{192,224},{1,3... | collective-permute-start | bytes 491528 | tf_op jit(solution)/shard_map/while/body/eval_jaxpr/ppermute | solution.py:19
  338.2 12.7 collective-permute-start
  365.5 16.6 %collective-permute-start = (bf16[2,8,8,640]{3,2,1,0:T(8,128)(2,1)S(1)}, bf16[2,8,8,640]{3,2,1,0:T(8,128)(2,1)}, u32[]{:S(2)}, u32[]{:S(2)}) collective-permute-start(bf16[2,8,8,640]{3,2,1,0:T(8,128)(2,1)S(1)} %get-tuple-element.1155), channel_id=1, source_target_pairs={{0,32},{32,64},{64,96},{96,128},{128,160},{160,192},{192,224},{1,3... | collective-permute-start | bytes 491528 | tf_op jit(solution)/shard_map/while/body/eval_jaxpr/ppermute | solution.py:19
  403.2 778.1 %while.41 = (s32[]{:T(128)}, bf16[2,8,8,640]{3,2,1,0:T(8,128)(2,1)}, f32[49,640]{1,0:T(8,128)S(1)}, f32[640,2560]{1,0:T(8,128)}, f32[2560,640]{1,0:T(8,128)}, /*...) while((s32[]{:T(128)}, ...), condition=%wide.region_63.64_spmd.clone, body=%wide.region_7.63_spmd.clone.sunk | while | flops 2131804288 | bytes 130983528 | solution.py:215
  407.5 14.1 collective-permute-done.1
  435.2 17.3 %collective-permute-done.1 = bf16[2,8,8,640]{3,2,1,0:T(8,128)(2,1)} collective-permute-done((bf16[2,8,8,640]{3,2,1,0:T(8,128)(2,1)}, bf16[2,8,8,640]{3,2,1,0:T(8,128)(2,1)}, u32[]{:S(2)}, u32[]{:S(2)}) %collective-permute-start.1) | collective-permute-done | bytes 163872 | tf_op jit(solution)/shard_map/while/body/eval_jaxpr/ppermute | solution.py:19
  466.1 13.4 collective-permute-done.1
  483.8 359.0 %collective-permute-done.1 = bf16[2,8,8,640]{3,2,1,0:T(8,128)(2,1)} collective-permute-done((bf16[2,8,8,640]{3,2,1,0:T(8,128)(2,1)}, bf16[2,8,8,640]{3,2,1,0:T(8,128)(2,1)}, u32[]{:S(2)}, u32[]{:S(2)}) %collective-permute-start.1) | collective-permute-done | bytes 163872 | tf_op jit(solution)/shard_map/while/body/eval_jaxpr/ppermute | solution.py:19
  844.6 60.5 %conditional.6 = (bf16[2,8,8,640]{3,2,1,0:T(8,128)(2,1)}, f32[49,640]{1,0:T(8,128)S(1)}, f32[640,2560]{1,0:T(8,128)}, f32[2560,640]{1,0:T(8,128)}) conditional(s32[]{:T(128)} %convert_element_type.175, (f32[49,640]{1,0:T(8,128)S(1)}, f32[640,2560]{1,0:T(8,128)}, f32[2560,640]{1,0:T(8,128)}) %tuple.251, (pred[]{:T(512)}, s32[]{:T(128)}, ...), branch_computations={%region_8.8_spmd, %region_9.62_spmd} | conditional | flops 2131148928 | bytes 129667864 | solution.py:209
  913.7 60.5 %conditional.6 = (bf16[2,8,8,640]{3,2,1,0:T(8,128)(2,1)}, f32[49,640]{1,0:T(8,128)S(1)}, f32[640,2560]{1,0:T(8,128)}, f32[2560,640]{1,0:T(8,128)}) conditional(s32[]{:T(128)} %convert_element_type.175, (f32[49,640]{1,0:T(8,128)S(1)}, f32[640,2560]{1,0:T(8,128)}, f32[2560,640]{1,0:T(8,128)}) %tuple.251, (pred[]{:T(512)}, s32[]{:T(128)}, ...), branch_computations={%region_8.8_spmd, %region_9.62_spmd} | conditional | flops 2131148928 | bytes 129667864 | solution.py:209
  982.8 60.5 %conditional.6 = (bf16[2,8,8,640]{3,2,1,0:T(8,128)(2,1)}, f32[49,640]{1,0:T(8,128)S(1)}, f32[640,2560]{1,0:T(8,128)}, f32[2560,640]{1,0:T(8,128)}) conditional(s32[]{:T(128)} %convert_element_type.175, (f32[49,640]{1,0:T(8,128)S(1)}, f32[640,2560]{1,0:T(8,128)}, f32[2560,640]{1,0:T(8,128)}) %tuple.251, (pred[]{:T(512)}, s32[]{:T(128)}, ...), branch_computations={%region_8.8_spmd, %region_9.62_spmd} | conditional | flops 2131148928 | bytes 129667864 | solution.py:209
  1051.9 60.5 %conditional.6 = (bf16[2,8,8,640]{3,2,1,0:T(8,128)(2,1)}, f32[49,640]{1,0:T(8,128)S(1)}, f32[640,2560]{1,0:T(8,128)}, f32[2560,640]{1,0:T(8,128)}) conditional(s32[]{:T(128)} %convert_element_type.175, (f32[49,640]{1,0:T(8,128)S(1)}, f32[640,2560]{1,0:T(8,128)}, f32[2560,640]{1,0:T(8,128)}) %tuple.251, (pred[]{:T(512)}, s32[]{:T(128)}, ...), branch_computations={%region_8.8_spmd, %region_9.62_spmd} | conditional | flops 2131148928 | bytes 129667864 | solution.py:209
  1121.6 58.4 %collective-permute-start.1 = (bf16[2,8,8,640]{3,2,1,0:T(8,128)(2,1)}, bf16[2,8,8,640]{3,2,1,0:T(8,128)(2,1)}, u32[]{:S(2)}, u32[]{:S(2)}) collective-permute-start(bf16[2,8,8,640]{3,2,1,0:T(8,128)(2,1)} %get-tuple-element.1053), channel_id=1, source_target_pairs={{32,0},{64,32},{96,64},{128,96},{160,128},{192,160},{224,192},{33,... | collective-permute-start | bytes 491528 | tf_op jit(solution)/shard_map/while/body/eval_jaxpr/ppermute | solution.py:19
  1191.4 83.6 %fusion.2 = bf16[24,2560]{1,0:T(8,128)(2,1)} fusion(bf16[640,2560]{1,0:T(8,128)(2,1)S(1)} %convert_element_type.133), kind=kCustom, calls=%all-reduce-scatter | all-reduce-scatter fusion | flops 1966081 | bytes 3400704
  1295.4 110.9 %psum.35 = bf16[1,49,640]{2,0,1:T(2,128)(2,1)S(1)} all-reduce(bf16[1,49,640]{2,0,1:T(2,128)(2,1)S(1)} %broadcast_in_dim.64), channel_id=1, replica_groups=mesh['section'=8,'dp'=32] {'dp'}, use_global_device_ids=true, to_apply=%region_66.67 | all-reduce | flops 31360 | bytes 125440 | tf_op jit(solution)/shard_map/psum | solution.py:226
  1408.3 54.4 %all-reduce.6 = (f32[640]{0:T(1024)S(1)}, f32[]{:T(128)}) all-reduce(f32[640]{0:T(1024)S(1)} %broadcast_multiply_fusion.4, f32[]{:T(128)S(6)} %mul.2377), channel_id=1, replica_groups=mesh['section'=8,'dp'=32] {'section'}, use_global_device_ids=true, to_apply=%region_68.69 | all-reduce | flops 641 | bytes 5128 | tf_op jit(solution)/shard_map/psum | solution.py:12
  1462.7 57.4 %all-reduce.5 = (f32[640]{0:T(1024)}, f32[]{:T(128)}) all-reduce(f32[640]{0:T(1024)S(1)} %get-tuple-element.886, f32[]{:T(128)} %get-tuple-element.887), channel_id=1, replica_groups=mesh['section'=8,'dp'=32] {'dp'}, use_global_device_ids=true, to_apply=%region_69.70 | all-reduce | flops 641 | bytes 5128 | tf_op jit(solution)/shard_map/psum | solution.py:13
  (1177 shorter events, 533.6 us)
Async XLA Ops:
  7.2 97.2 %all-gather.5.cloned.1.call-start = ((), (), s32[]{:S(2)}) async-start(), calls=%async_computation.2 | async-start | bytes 6758400 | tf_op jit(solution)/shard_map/all_gather | solution.py:140
  9.0 171.6 %all-gather.7.cloned.1.call-start = ((), (), s32[]{:S(2)}) async-start(), calls=%async_computation.3 | async-start | bytes 3379200 | tf_op jit(solution)/shard_map/all_gather | solution.py:141
  9.8 1512.7 %reduce-scatter.4.cloned.1.call-start = ((), (), s32[]{:S(2)}) async-start(), calls=%async_computation.1 | async-start | bytes 3379200 | tf_op jit(solution)/shard_map/reduce_scatter | solution.py:222
  185.9 21.6 %collective-permute-start = (bf16[2,8,8,640]{3,2,1,0:T(8,128)(2,1)S(1)}, bf16[2,8,8,640]{3,2,1,0:T(8,128)(2,1)}, u32[]{:S(2)}, u32[]{:S(2)}) collective-permute-start(bf16[2,8,8,640]{3,2,1,0:T(8,128)(2,1)S(1)} %get-tuple-element.1155), channel_id=1, source_target_pairs={{0,32},{32,64},{64,96},{96,128},{128,160},{160,192},{192,224},{1,3... | collective-permute-start | bytes 491528 | tf_op jit(solution)/shard_map/while/body/eval_jaxpr/ppermute | solution.py:19
  304.5 21.4 %collective-permute-start = (bf16[2,8,8,640]{3,2,1,0:T(8,128)(2,1)S(1)}, bf16[2,8,8,640]{3,2,1,0:T(8,128)(2,1)}, u32[]{:S(2)}, u32[]{:S(2)}) collective-permute-start(bf16[2,8,8,640]{3,2,1,0:T(8,128)(2,1)S(1)} %get-tuple-element.1155), channel_id=1, source_target_pairs={{0,32},{32,64},{64,96},{96,128},{128,160},{160,192},{192,224},{1,3... | collective-permute-start | bytes 491528 | tf_op jit(solution)/shard_map/while/body/eval_jaxpr/ppermute | solution.py:19
  338.2 14.9 collective-permute-start
  365.5 18.8 %collective-permute-start = (bf16[2,8,8,640]{3,2,1,0:T(8,128)(2,1)S(1)}, bf16[2,8,8,640]{3,2,1,0:T(8,128)(2,1)}, u32[]{:S(2)}, u32[]{:S(2)}) collective-permute-start(bf16[2,8,8,640]{3,2,1,0:T(8,128)(2,1)S(1)} %get-tuple-element.1155), channel_id=1, source_target_pairs={{0,32},{32,64},{64,96},{96,128},{128,160},{160,192},{192,224},{1,3... | collective-permute-start | bytes 491528 | tf_op jit(solution)/shard_map/while/body/eval_jaxpr/ppermute | solution.py:19
  405.6 16.0 %collective-permute-start.1 = (bf16[2,8,8,640]{3,2,1,0:T(8,128)(2,1)}, bf16[2,8,8,640]{3,2,1,0:T(8,128)(2,1)}, u32[]{:S(2)}, u32[]{:S(2)}) collective-permute-start(bf16[2,8,8,640]{3,2,1,0:T(8,128)(2,1)} %get-tuple-element.1053), channel_id=1, source_target_pairs={{32,0},{64,32},{96,64},{128,96},{160,128},{192,160},{224,192},{33,... | collective-permute-start | bytes 491528 | tf_op jit(solution)/shard_map/while/body/eval_jaxpr/ppermute | solution.py:19
  423.9 6.9 collective-permute-start.1
  433.3 19.2 %collective-permute-start.1 = (bf16[2,8,8,640]{3,2,1,0:T(8,128)(2,1)}, bf16[2,8,8,640]{3,2,1,0:T(8,128)(2,1)}, u32[]{:S(2)}, u32[]{:S(2)}) collective-permute-start(bf16[2,8,8,640]{3,2,1,0:T(8,128)(2,1)} %get-tuple-element.1053), channel_id=1, source_target_pairs={{32,0},{64,32},{96,64},{128,96},{160,128},{192,160},{224,192},{33,... | collective-permute-start | bytes 491528 | tf_op jit(solution)/shard_map/while/body/eval_jaxpr/ppermute | solution.py:19
  454.9 6.9 collective-permute-start.1
  464.2 15.3 %collective-permute-start.1 = (bf16[2,8,8,640]{3,2,1,0:T(8,128)(2,1)}, bf16[2,8,8,640]{3,2,1,0:T(8,128)(2,1)}, u32[]{:S(2)}, u32[]{:S(2)}) collective-permute-start(bf16[2,8,8,640]{3,2,1,0:T(8,128)(2,1)} %get-tuple-element.1053), channel_id=1, source_target_pairs={{32,0},{64,32},{96,64},{128,96},{160,128},{192,160},{224,192},{33,... | collective-permute-start | bytes 491528 | tf_op jit(solution)/shard_map/while/body/eval_jaxpr/ppermute | solution.py:19
  481.9 360.9 %collective-permute-start.1 = (bf16[2,8,8,640]{3,2,1,0:T(8,128)(2,1)}, bf16[2,8,8,640]{3,2,1,0:T(8,128)(2,1)}, u32[]{:S(2)}, u32[]{:S(2)}) collective-permute-start(bf16[2,8,8,640]{3,2,1,0:T(8,128)(2,1)} %get-tuple-element.1053), channel_id=1, source_target_pairs={{32,0},{64,32},{96,64},{128,96},{160,128},{192,160},{224,192},{33,... | collective-permute-start | bytes 491528 | tf_op jit(solution)/shard_map/while/body/eval_jaxpr/ppermute | solution.py:19
  905.0 6.9 collective-permute-start.1
  974.1 6.9 collective-permute-start.1
  1043.2 6.9 collective-permute-start.1
  1112.3 6.9 collective-permute-start.1
  1121.6 59.7 %collective-permute-start.1 = (bf16[2,8,8,640]{3,2,1,0:T(8,128)(2,1)}, bf16[2,8,8,640]{3,2,1,0:T(8,128)(2,1)}, u32[]{:S(2)}, u32[]{:S(2)}) collective-permute-start(bf16[2,8,8,640]{3,2,1,0:T(8,128)(2,1)} %get-tuple-element.1053), channel_id=1, source_target_pairs={{32,0},{64,32},{96,64},{128,96},{160,128},{192,160},{224,192},{33,... | collective-permute-start | bytes 491528 | tf_op jit(solution)/shard_map/while/body/eval_jaxpr/ppermute | solution.py:19
  1275.8 244.3 %collective-permute-start.6 = (bf16[24,2560]{1,0:T(8,128)(2,1)}, bf16[24,2560]{1,0:T(8,128)(2,1)S(1)}, u32[]{:S(2)}, u32[]{:S(2)}) collective-permute-start(bf16[24,2560]{1,0:T(8,128)(2,1)} %fusion.2), channel_id=1, source_target_pairs={{0,5},{1,6},{2,7},{3,8},{4,9},{5,10},{6,11},{7,12},{8,13},{9,14},{... | collective-permute-start | bytes 368648
  1277.2 243.0 %collective-permute-start.5 = (bf16[24,2560]{1,0:T(8,128)(2,1)}, bf16[24,2560]{1,0:T(8,128)(2,1)S(1)}, u32[]{:S(2)}, u32[]{:S(2)}) collective-permute-start(bf16[24,2560]{1,0:T(8,128)(2,1)} %fusion.2), channel_id=1, source_target_pairs={{0,4},{1,5},{2,6},{3,7},{4,8},{5,9},{6,10},{7,11},{8,12},{9,13},{1... | collective-permute-start | bytes 368648
  1278.7 241.5 %collective-permute-start.4 = (bf16[24,2560]{1,0:T(8,128)(2,1)}, bf16[24,2560]{1,0:T(8,128)(2,1)S(1)}, u32[]{:S(2)}, u32[]{:S(2)}) collective-permute-start(bf16[24,2560]{1,0:T(8,128)(2,1)} %fusion.2), channel_id=1, source_target_pairs={{0,3},{1,4},{2,5},{3,6},{4,7},{5,8},{6,9},{7,10},{8,11},{9,12},{10... | collective-permute-start | bytes 368648
  1280.0 240.2 %collective-permute-start.3 = (bf16[24,2560]{1,0:T(8,128)(2,1)}, bf16[24,2560]{1,0:T(8,128)(2,1)S(1)}, u32[]{:S(2)}, u32[]{:S(2)}) collective-permute-start(bf16[24,2560]{1,0:T(8,128)(2,1)} %fusion.2), channel_id=1, source_target_pairs={{0,2},{1,3},{2,4},{3,5},{4,6},{5,7},{6,8},{7,9},{8,10},{9,11},{10,... | collective-permute-start | bytes 368648
  1283.7 123.4 %collective-permute-start.7 = (bf16[4,2560]{1,0:T(4,128)(2,1)S(1)}, bf16[4,2560]{1,0:T(4,128)(2,1)S(1)}, u32[]{:S(2)}, u32[]{:S(2)}) collective-permute-start(bf16[4,2560]{1,0:T(4,128)(2,1)S(1)} %slice.1262), channel_id=1, source_target_pairs={{0,6},{1,7},{2,8},{3,9},{4,10},{5,11},{6,12},{7,13},{8,14},{9,15},... | collective-permute-start | bytes 61448
  1407.0 113.1 %collective-permute-start.2 = (bf16[24,2560]{1,0:T(8,128)(2,1)S(1)}, bf16[24,2560]{1,0:T(8,128)(2,1)S(1)}, u32[]{:S(2)}, u32[]{:S(2)}) collective-permute-start(bf16[24,2560]{1,0:T(8,128)(2,1)S(1)} %copy-done.77), channel_id=1, source_target_pairs={{0,1},{1,2},{2,3},{3,4},{4,5},{5,6},{6,7},{7,8},{8,9},{9,10},{10,1... | collective-permute-start | bytes 368648
  (339 other events, 1251.0 us)
Sparse Core Ops, SparseCore 0:
  11.2 93.1 all-gather.4
  107.0 73.6 all-gather.6
  1186.4 195.3 reduce-scatter.3
